TPU v7x, 128 devices: a whole 4x4x4 slice. The times are simulated.
128 devices in a mesh: rows: 32 (over x, z, core), cols: 4 (over y).
Axes of the slice: x: 4, y: 4, z: 4, core: 2. Of those that a mesh axis runs over, the one named last changes fastest.
Arguments:
- table: bfloat16 [262144, 512], P('rows', 'cols'), may hold values from -6 to 6
- item_ids: int32 [256, 256], P(('rows', 'cols')), may hold values from 0 to 262143, as said below
- cotangent: bfloat16 [256, 256, 512], P(('rows', 'cols')), may hold values from -6 to 6
- norm_gain: float32 [512], replicated, may hold values from 0.25 to 1.75
- w_in: bfloat16 [512, 2048], replicated, may hold values from -0.25 to 0.25
- bias_in: float32 [2048], replicated, may hold values from -3 to 3
- w_out: bfloat16 [2048, 512], replicated, may hold values from -0.125 to 0.125
Outputs:
- table_grad: float32 [262144, 512], P('rows', 'cols')
- w_in_grad: float32 [512, 2048], replicated
- bias_grad: float32 [2048], replicated
- w_out_grad: float32 [2048, 512], replicated
- gain_grad: float32 [512], replicated
Inputs may be any that keep to these rules, and one draw needn't show every extreme that they name: `item_ids`: within each device's 512 positions (aligned blocks of 2 sequences), at most 32 name rows of one range k * 8192 to (k + 1) * 8192 - 1; one range is named by exactly 32 positions of every device.
All inputs are finite; a program needn't handle non-finite values.
Results may differ from a plain program's by a relative error of at most 0.0051.
Values may be sent and summed in bfloat16 or wider, within the bound.
No kernel may reach another device: no remote copies, remote signals or barrier semaphores. Data moves between devices by JAX's collectives and lax.ppermute only.
A program may use at most 128 MiB of HBM per device.

v0:
```python
import math
import jax
import jax.numpy as jnp
from jax import lax
from jax.sharding import PartitionSpec as P

norm_eps = 1e-06
gelu_coef = 0.7978845608


def local_pass(embedded, d_out, norm_gain, w_in, bias_in, w_out):
    x_float = embedded.astype(jnp.float32)
    inv_rms = lax.rsqrt(jnp.mean(x_float * x_float, axis=-1, keepdims=True) + norm_eps)
    x_hat = x_float * inv_rms
    normed = (x_hat * norm_gain).astype(jnp.bfloat16)
    pre_act = jnp.dot(normed, w_in, preferred_element_type=jnp.float32) + bias_in
    tanh_part = jnp.tanh(gelu_coef * (pre_act + 0.044715 * pre_act * pre_act * pre_act))
    hidden = (0.5 * pre_act * (1.0 + tanh_part)).astype(jnp.bfloat16)
    d_act = lax.dot_general(
        d_out, w_out, (((1,), (1,)), ((), ())), preferred_element_type=jnp.float32
    )
    slope = 0.5 * (1.0 + tanh_part) + 0.5 * pre_act * (1.0 - tanh_part * tanh_part) * gelu_coef * (
        1.0 + 3.0 * 0.044715 * pre_act * pre_act
    )
    d_pre = d_act * slope
    d_pre_bf = d_pre.astype(jnp.bfloat16)
    g_out = lax.dot_general(
        hidden, d_out, (((0,), (0,)), ((), ())), preferred_element_type=jnp.float32
    )
    g_in = lax.dot_general(
        normed, d_pre_bf, (((0,), (0,)), ((), ())), preferred_element_type=jnp.float32
    )
    g_bias = jnp.sum(d_pre, axis=0)
    d_norm = lax.dot_general(
        d_pre_bf, w_in, (((1,), (1,)), ((), ())), preferred_element_type=jnp.float32
    )
    g_gain = jnp.sum(d_norm * x_hat, axis=0)
    scaled = d_norm * norm_gain
    d_embed = inv_rms * (
        scaled - x_hat * jnp.mean(scaled * x_hat, axis=-1, keepdims=True)
    ) + d_out.astype(jnp.float32)
    return (d_embed, g_in, g_bias, g_out, g_gain)


def local(table, item_ids, cotangent, norm_gain, w_in, bias_in, w_out):
    n_rows = lax.axis_size("rows")
    n_cols = lax.axis_size("cols")
    rows_dev = table.shape[0]
    col_width = table.shape[1]
    flat_ids = item_ids.reshape(-1)
    n_tokens = flat_ids.shape[0]
    capacity = max(2, 2 * n_tokens // n_rows)
    owners = flat_ids // rows_dev
    offsets = flat_ids - owners * rows_dev
    range_ids = jnp.arange(n_rows, dtype=jnp.int32)
    onehot = (owners[:, None] == range_ids[None, :]).astype(jnp.float32)
    tok_ids = jnp.arange(n_tokens, dtype=jnp.int32)
    lower = (tok_ids[:, None] >= tok_ids[None, :]).astype(jnp.float32)
    running = jnp.dot(lower, onehot, preferred_element_type=jnp.float32)
    rank_tok = (jnp.sum(running * onehot, axis=1) - 1.0).astype(jnp.int32)
    slot_of = owners * capacity + rank_tok
    n_slots = n_rows * capacity
    slot_ids = jnp.arange(n_slots, dtype=jnp.int32)
    slot_hit = slot_of[:, None] == slot_ids[None, :]
    wanted = jnp.sum(jnp.where(slot_hit, offsets[:, None], 0), axis=0).reshape(n_rows, capacity)
    requests = jnp.broadcast_to(wanted[:, None, :], (n_rows, n_cols, capacity)).reshape(
        n_rows * n_cols, capacity
    )
    looked = jnp.take(
        table,
        lax.all_to_all(requests, ("rows", "cols"), split_axis=0, concat_axis=0, tiled=True),
        axis=0,
    )
    fetched = lax.all_to_all(looked, ("rows", "cols"), split_axis=0, concat_axis=0, tiled=True)
    width = n_cols * col_width
    by_slot = jnp.transpose(
        fetched.reshape(n_rows, n_cols, capacity, col_width), (0, 2, 1, 3)
    ).reshape(n_slots, width)
    embedded = jnp.dot(
        slot_hit.astype(jnp.bfloat16), by_slot, preferred_element_type=jnp.float32
    ).astype(jnp.bfloat16)
    d_out = cotangent.reshape(n_tokens, width)
    block_rows = 512
    n_blocks = n_tokens // block_rows
    ff_width = w_in.shape[1]

    def one_block(carry, block):
        acc_in, acc_bias, acc_out, acc_gain = carry
        d_embed, g_in, g_bias, g_out, g_gain = local_pass(
            block[0], block[1], norm_gain, w_in, bias_in, w_out
        )
        return ((acc_in + g_in, acc_bias + g_bias, acc_out + g_out, acc_gain + g_gain), d_embed)

    start = (
        jnp.zeros((width, ff_width), jnp.float32),
        jnp.zeros((ff_width,), jnp.float32),
        jnp.zeros((ff_width, width), jnp.float32),
        jnp.zeros((width,), jnp.float32),
    )
    totals, d_blocks = lax.scan(
        one_block,
        start,
        (embedded.reshape(n_blocks, block_rows, width), d_out.reshape(n_blocks, block_rows, width)),
    )
    g_in, g_bias, g_out, g_gain = totals
    d_embed = d_blocks.reshape(n_tokens, width)
    slot_grad = lax.dot_general(
        slot_hit.astype(jnp.float32),
        d_embed,
        (((0,), (0,)), ((), ())),
        precision=lax.Precision.HIGHEST,
        preferred_element_type=jnp.float32,
    )
    payload = jnp.transpose(slot_grad.reshape(n_rows, capacity, n_cols, col_width), (0, 2, 1, 3))
    arrived, arrived_off = (
        lax.all_to_all(
            payload.reshape(n_rows * n_cols, capacity, col_width),
            ("rows", "cols"),
            split_axis=0,
            concat_axis=0,
            tiled=True,
        ),
        lax.all_to_all(requests, ("rows", "cols"), split_axis=0, concat_axis=0, tiled=True),
    )
    table_grad = (
        jnp.zeros((rows_dev, col_width), jnp.float32)
        .at[arrived_off.reshape(-1)]
        .add(arrived.reshape(-1, col_width))
    )
    summed = lax.psum((g_in, g_bias, g_out, g_gain), ("rows", "cols"))
    scale = 1.0 / math.sqrt(n_tokens * n_rows * n_cols)
    return (table_grad, summed[0] * scale, summed[1] * scale, summed[2] * scale, summed[3] * scale)


def solution(mesh):
    return jax.shard_map(
        local,
        mesh=mesh,
        in_specs=(
            P("rows", "cols"),
            P(("rows", "cols"), None),
            P(("rows", "cols"), None, None),
            P(),
            P(),
            P(),
            P(),
        ),
        out_specs=(P("rows", "cols"), P(), P(), P(), P()),
        check_vma=False,
    )
```

profile of v0, /device:TPU:1, one launch (start us, length us, event | category | flops | bytes accessed | tf_op | source)
XLA Modules:
  0.0 274.7 jit_solution(9714781316654998836)
XLA Ops:
  7.2 0.0 copy-start
  7.2 0.0 all-reduce.4.cloned.1.call-start
  7.2 0.8 copy.22
  8.1 0.3 fusion.18
  8.4 0.3 select_reduce_fusion
  8.6 0.1 broadcast_in_dim.60
  8.7 21.2 %all_to_all.26 = s32[128,1,32]{2,1,0:T(1,128)S(1)} all-to-all(s32[128,1,32]{2,1,0:T(1,128)S(1)} %bitcast.52), channel_id=1, replica_groups=mesh['rows'=32,'cols'=4] {'rows','cols'}, dimensions={0} | all-to-all | bytes 32768 | tf_op jit(solution)/shard_map/all_to_all | solution.py:123
  30.0 0.1 reshape.200
  30.1 12.9 %gather_fusion = bf16[4096,128]{1,0:T(8,128)(2,1)S(1)} fusion(bf16[8192,128]{1,0:T(8,128)(2,1)} %param.7, s32[4096]{0:T(1024)S(1)} %broadcast_clamp_fusion), kind=kCustom, calls=%fused_computation | custom fusion | bytes 2113536 | tf_op jit(solution)/shard_map/jit(_take)/gather | solution.py:69
  43.0 0.8 broadcast_select_fusion
  43.8 0.0 copy-start.4
  43.8 23.5 %all_to_all.27 = bf16[128,32,128]{2,1,0:T(8,128)(2,1)S(1)} all-to-all(bf16[128,32,128]{2,1,0:T(8,128)(2,1)S(1)} %broadcast_select_fusion), channel_id=1, replica_groups=mesh['rows'=32,'cols'=4] {'rows','cols'}, dimensions={0} | all-to-all | bytes 2097152 | tf_op jit(solution)/shard_map/all_to_all | solution.py:74
  67.3 0.5 copy.18
  67.8 0.9 fusion.25
  68.8 0.0 copy-start.3
  68.8 0.0 copy-start.6
  68.8 0.0 copy-done
  68.8 0.0 copy-done.4
  68.8 1.4 fusion.36
  70.2 0.0 copy-done.3
  70.2 0.0 copy-done.6
  70.2 0.0 copy-start.5
  70.2 4.2 %fusion.9 = f32[2048,512]{1,0:T(8,128)} fusion(bf16[512,512]{1,0:T(8,128)(2,1)S(1)} %bitcast.50, f32[512,2048]{1,0:T(8,128)S(1)} %fusion.36, f32[2048]{0:T(1024)S(1)} %copy-done.6), kind=kOutput, calls=%fused_computation.18 | convolution fusion | flops 1084227584 | bytes 8921088 | tf_op jit(solution)/shard_map/while/body/eval_jaxpr/dot_general | solution.py:27
  74.4 0.0 copy-done.5
  74.4 3.6 %fusion.45 = (f32[2048]{0:T(1024)S(1)}, bf16[512,2048]{1,0:T(8,128)(2,1)S(1)}) fusion(f32[512,2048]{1,0:T(8,128)S(1)} %fusion.36, f32[2048]{0:T(1024)S(1)} %copy-done.6, bf16[512,512]{1,0:T(8,128)(2,1)S(1)} %bitcast.51, bf16[2048,512]{1,0:T(8,128)(2,1)S(1)} %copy-done.5), kind=kOutput, calls=%fused_computation.75 | convolution fusion | flops 1095759872 | bytes 8929280 | tf_op jit(solution)/shard_map/while/body/eval_jaxpr/dot_general | solution.py:19
  78.0 0.0 copy-start.2
  78.0 1.3 copy-done.2
  79.3 3.3 %fusion.28 = f32[512,2048]{1,0:T(8,128)} fusion(bf16[512,2048]{1,0:T(8,128)(2,1)S(1)} %get-tuple-element.53, bf16[512,512]{0,1:T(8,128)(2,1)S(1)} %get-tuple-element.50, f32[512]{0:T(512)S(1)} %copy-done.4, f32[512]{0:T(512)S(1)} %add_rsqrt_fusion), kind=kOutput, calls=%fused_computation.40 | convolution fusion | flops 1074790400 | bytes 6819840 | tf_op jit(solution)/shard_map/while/body/eval_jaxpr/dot_general | solution.py:30
  82.6 0.0 all-reduce.4.cloned.1.call-update
  82.7 1.3 copy.21
  83.9 3.0 %fusion.24 = (f32[512]{0:T(512)S(1)}, f32[512]{0:T(512)S(1)}, f32[512,512]{0,1:T(8,128)S(1)}) fusion(bf16[512,512]{0,1:T(8,128)(2,1)S(1)} %get-tuple-element.50, f32[512]{0:T(512)S(1)} %add_rsqrt_fusion, f32[512]{0:T(512)S(1)} %copy-done.4, bf16[512,2048]{1,0:T(8,128)(2,1)S(1)} %copy-done, bf16[512,2048]{1,0:T(8,128)(2,1)} %copy-done.2), kind=kOutput, calls=%fused_computation.36 | convolution fusion | flops 1075575808 | bytes 5775360 | tf_op jit(solution)/shard_map/while/body/eval_jaxpr/dot_general | solution.py:34
  87.0 0.3 fusion.23
  87.3 3.2 %fusion.10 = f32[32,32,4,128]{3,1,2,0:T(8,128)} fusion(f32[4,128,512,1]{2,1,0,3:T(8,128)S(1)} %bitcast.45, s32[32,32]{1,0:T(8,128)S(1)} %multiply_add_fusion.1, s32[512]{0:T(512)S(1)} %convert_add_fusion), kind=kOutput, calls=%fused_computation.19 | convolution fusion | flops 3221749760 | bytes 3151872 | tf_op jit(solution)/shard_map/dot_general | solution.py:107
  90.5 4.8 %all-to-all-start.2 = ((f32[128,32,128]{2,1,0:T(8,128)}), f32[128,32,128]{2,1,0:T(8,128)}, u32[]{:S(2)}, u32[]{:S(2)}) async-start(f32[128,32,128]{2,1,0:T(8,128)} %bitcast.42), calls=%async_computation.2 | async-start | bytes 4194304 | tf_op jit(solution)/shard_map/all_to_all | solution.py:116
  95.3 0.5 broadcast.230
  95.8 0.8 reduce.3
  96.7 0.1 reshape.193
  96.8 85.3 %all-reduce = (f32[2048]{0:T(1024)S(1)}, f32[512]{0:T(512)S(1)}) all-reduce(f32[2048]{0:T(1024)S(1)} %get-tuple-element.52, f32[512]{0:T(512)S(1)} %get-tuple-element.29), channel_id=1, replica_groups=mesh['rows'=32,'cols'=4] {'rows','cols'}, use_global_device_ids=true, to_apply=%region_7.8 | all-reduce | flops 2560 | bytes 20480 | tf_op jit(solution)/shard_map/psum | solution.py:130
  182.1 0.6 broadcast_multiply_fusion.3
  182.7 0.6 broadcast_multiply_fusion.2
  183.3 0.0 all-to-all-done.2
  183.3 25.4 %scatter_custom_fusion = f32[8192,128]{1,0:T(8,128)} fusion(s32[4096]{0:T(1024)S(1)} %bitcast.53, f32[4096,128]{1,0:T(8,128)} %bitcast.15, f32[]{:T(128)} %constant.40.clone.1), kind=kCustom, calls=%fused_computation.16 | custom fusion | flops 524288 | bytes 4194816 | tf_op jit(solution)/shard_map/scatter-add | solution.py:128
  208.7 51.7 %all-reduce.4.cloned.1.call-done = (f32[512,2048]{1,0:T(8,128)}, f32[2048,512]{1,0:T(8,128)}) async-done(((f32[512,2048]{1,0:T(8,128)}, f32[2048,512]{1,0:T(8,128)}), (f32[512,2048]{1,0:T(8,128)}, f32[2048,512]{1,0:T(8,128)})) %all-reduce.4.cloned.1.call-update) | async-done | bytes 8388624 | tf_op jit(solution)/shard_map/psum | solution.py:130
  260.4 0.0 copy-start.1
  260.4 4.9 %broadcast_multiply_fusion.1 = f32[512,2048]{1,0:T(8,128)} fusion(f32[512,2048]{1,0:T(8,128)} %get-tuple-element.33), kind=kLoop, calls=%fused_computation.12 | loop fusion | flops 1048576 | bytes 8388608 | tf_op jit(solution)/shard_map/mul | solution.py:132
  265.3 0.0 copy-done.1
  265.3 2.5 broadcast_multiply_fusion
  (10 shorter events, 0.1 us)
Async XLA Ops:
  7.2 61.6 %copy-start = (bf16[512,2048]{1,0:T(8,128)(2,1)S(1)}, bf16[512,2048]{1,0:T(8,128)(2,1)}, u32[]{:S(2)}) copy-start(bf16[512,2048]{1,0:T(8,128)(2,1)} %param.11) | copy-start | bytes 6291460
  7.2 253.2 %all-reduce.4.cloned.1.call-start = ((), (), s32[]{:S(2)}) async-start(), calls=%async_computation.3 | async-start | bytes 16777216 | tf_op jit(solution)/shard_map/psum | solution.py:130
  43.8 25.0 %copy-start.4 = (f32[512]{0:T(512)S(1)}, f32[512]{0:T(512)}, u32[]{:S(2)}) copy-start(f32[512]{0:T(512)} %param.10) | copy-start | bytes 6148
  68.8 1.4 copy-start.3
  68.8 1.4 copy-start.6
  70.2 4.2 %copy-start.5 = (bf16[2048,512]{1,0:T(8,128)(2,1)S(1)}, bf16[2048,512]{1,0:T(8,128)(2,1)}, u32[]{:S(2)}) copy-start(bf16[2048,512]{1,0:T(8,128)(2,1)} %param.13) | copy-start | bytes 6291460
  78.0 1.3 copy-start.2
  90.5 92.8 %all-to-all-start.2 = ((f32[128,32,128]{2,1,0:T(8,128)}), f32[128,32,128]{2,1,0:T(8,128)}, u32[]{:S(2)}, u32[]{:S(2)}) async-start(f32[128,32,128]{2,1,0:T(8,128)} %bitcast.42), calls=%async_computation.2 | async-start | bytes 4194304 | tf_op jit(solution)/shard_map/all_to_all | solution.py:116
  260.4 4.9 %copy-start.1 = (f32[2048,512]{1,0:T(8,128)S(1)}, f32[2048,512]{1,0:T(8,128)}, u32[]{:S(2)}) copy-start(f32[2048,512]{1,0:T(8,128)} %get-tuple-element.34) | copy-start | bytes 12582916
Sparse Core Ops, SparseCore 0:
  82.8 177.5 all-reduce.3
where the time goes:
time: 275 us
  blocking collectives  130 us (47%)
  waiting for transfers between devices  51.7 us (19%)
  other arithmetic  36.3 us (13%)
  matrix products  19.9 us (7%)
  local copies, waits for them, and re-layouts  17.6 us (6%)
  between operations  14.2 us (5%)
  starting transfers between devices  4.84 us (2%)
    psum x1, blocking collectives, local(): summed = lax.psum((g_in, g_bias, g_out, g_gain), ('rows', 'cols'))  85.3 us
    psum x1, waiting for transfers between devices, local(): summed = lax.psum((g_in, g_bias, g_out, g_gain), ('rows', 'cols'))  51.7 us
    scatter-add x1, other arithmetic, local(): table_grad = jnp.zeros((rows_dev, col_width), jnp.float32).at[arrived_off...  25.4 us
    all_to_all x1, blocking collectives, local(): lax.all_to_all(looked, ('rows', 'cols'), split_axis=0, concat_axis=0, til...  23.5 us
    all_to_all x1, blocking collectives, local(): lax.all_to_all(requests, ('rows', 'cols'), split_axis=0, concat_axis=0, t...  21.2 us
    gather x1, local copies, waits for them, and re-layouts, local(): jnp.take(table, lax.all_to_all(requests, ('rows', 'cols'), split_axis=0,...  12.9 us
  transfers between devices with their start and end apart: 2, of which 1 were waited for; matrix products, arithmetic and copies ran while one was open for 13% of the time, Pallas kernels for 0%

commit v1 on v0

--- a/solution.py
+++ b/solution.py
@@ -127,7 +127,7 @@
         .at[arrived_off.reshape(-1)]
         .add(arrived.reshape(-1, col_width))
     )
-    summed = lax.psum((g_in, g_bias, g_out, g_gain), ("rows", "cols"))
+    summed = lax.psum(lax.psum((g_in, g_bias, g_out, g_gain), "rows"), "cols")
     scale = 1.0 / math.sqrt(n_tokens * n_rows * n_cols)
     return (table_grad, summed[0] * scale, summed[1] * scale, summed[2] * scale, summed[3] * scale)
 

time: 275 us -> 416 us (1.51); the launches traced: 275 us -> 409 us
  blocking collectives: 130 us -> 197 us
  waiting for transfers between devices: 51.7 us -> 116 us
    psum x1 -> x2, blocking collectives: 85.3 us -> 152 us  [local(): summed = lax.psum(lax.psum((g_in, g_bias, g_out, g_gain), 'rows'), 'cols')]
    psum x1 -> x2, waiting for transfers between devices: 51.7 us -> 116 us  [local(): summed = lax.psum(lax.psum((g_in, g_bias, g_out, g_gain), 'rows'), 'cols')]
  transfers between devices with their start and end apart: 2 -> 3, of which waited for: 1 -> 1; matrix products, arithmetic and copies ran while one was open for 13% -> 9% of each run, Pallas kernels for 0% -> 0%
where the time goes in v1:
time: 416 us; the launch traced here: 409 us
  blocking collectives  197 us (47%)
  waiting for transfers between devices  116 us (28%)
  other arithmetic  36.1 us (9%)
  matrix products  19.9 us (5%)
  local copies, waits for them, and re-layouts  17.6 us (4%)
  between operations  14.3 us (3%)
  starting transfers between devices  8.65 us (2%)
    psum x2, blocking collectives, local(): summed = lax.psum(lax.psum((g_in, g_bias, g_out, g_gain), 'rows'), 'cols')  152 us
    psum x2, waiting for transfers between devices, local(): summed = lax.psum(lax.psum((g_in, g_bias, g_out, g_gain), 'rows'), 'cols')  116 us
    scatter-add x1, other arithmetic, local(): table_grad = jnp.zeros((rows_dev, col_width), jnp.float32).at[arrived_off...  25.4 us
    all_to_all x1, blocking collectives, local(): lax.all_to_all(looked, ('rows', 'cols'), split_axis=0, concat_axis=0, til...  23.5 us
    all_to_all x1, blocking collectives, local(): lax.all_to_all(requests, ('rows', 'cols'), split_axis=0, concat_axis=0, t...  21.2 us
    gather x1, local copies, waits for them, and re-layouts, local(): jnp.take(table, lax.all_to_all(requests, ('rows', 'cols'), split_axis=0,...  12.9 us
    all_to_all x1, starting transfers between devices, local(): lax.all_to_all(payload.reshape(n_rows * n_cols, capacity, col_width), ('r...  8.39 us
  transfers between devices with their start and end apart: 3, of which 1 were waited for; matrix products, arithmetic and copies ran while one was open for 9% of the time, Pallas kernels for 0%

profile of v1, /device:TPU:1, one launch (start us, length us, event | category | flops | bytes accessed | tf_op | source)
XLA Modules:
  0.0 409.1 jit_solution(12482663006456205413)
XLA Ops:
  7.2 0.0 copy-start
  7.2 0.0 all-reduce.7.cloned.1.call-start
  7.2 0.8 copy.22
  8.1 0.3 fusion.18
  8.4 0.3 select_reduce_fusion
  8.6 0.1 broadcast_in_dim.60
  8.7 21.2 %all_to_all.26 = s32[128,1,32]{2,1,0:T(1,128)S(1)} all-to-all(s32[128,1,32]{2,1,0:T(1,128)S(1)} %bitcast.52), channel_id=1, replica_groups=mesh['rows'=32,'cols'=4] {'rows','cols'}, dimensions={0} | all-to-all | bytes 32768 | tf_op jit(solution)/shard_map/all_to_all | solution.py:123
  29.9 0.1 reshape.200
  30.1 12.9 %gather_fusion = bf16[4096,128]{1,0:T(8,128)(2,1)S(1)} fusion(bf16[8192,128]{1,0:T(8,128)(2,1)} %param.7, s32[4096]{0:T(1024)S(1)} %broadcast_clamp_fusion), kind=kCustom, calls=%fused_computation | custom fusion | bytes 2113536 | tf_op jit(solution)/shard_map/jit(_take)/gather | solution.py:69
  43.0 0.8 broadcast_select_fusion
  43.8 0.0 copy-start.4
  43.8 23.5 %all_to_all.27 = bf16[128,32,128]{2,1,0:T(8,128)(2,1)S(1)} all-to-all(bf16[128,32,128]{2,1,0:T(8,128)(2,1)S(1)} %broadcast_select_fusion), channel_id=1, replica_groups=mesh['rows'=32,'cols'=4] {'rows','cols'}, dimensions={0} | all-to-all | bytes 2097152 | tf_op jit(solution)/shard_map/all_to_all | solution.py:74
  67.3 0.5 copy.18
  67.8 0.9 fusion.25
  68.8 0.0 copy-start.3
  68.8 0.0 copy-start.6
  68.8 0.0 copy-done
  68.8 0.0 copy-done.4
  68.8 1.4 fusion.36
  70.2 0.0 copy-done.3
  70.2 0.0 copy-done.6
  70.2 0.0 copy-start.5
  70.2 4.2 %fusion.9 = f32[2048,512]{1,0:T(8,128)} fusion(bf16[512,512]{1,0:T(8,128)(2,1)S(1)} %bitcast.50, f32[512,2048]{1,0:T(8,128)S(1)} %fusion.36, f32[2048]{0:T(1024)S(1)} %copy-done.6), kind=kOutput, calls=%fused_computation.18 | convolution fusion | flops 1084227584 | bytes 8921088 | tf_op jit(solution)/shard_map/while/body/eval_jaxpr/dot_general | solution.py:27
  74.4 0.0 copy-done.5
  74.4 3.6 fusion.45
  78.0 0.0 copy-start.2
  78.0 1.3 copy-done.2
  79.3 3.3 fusion.28
  82.6 0.0 all-reduce.7.cloned.1.call-update
  82.7 0.2 all-reduce.9.cloned.1.call-start
  82.9 116.0 %all-reduce.7.cloned.1.call-done = (f32[512,2048]{1,0:T(8,128)}, f32[2048,512]{1,0:T(8,128)}) async-done(((f32[512,2048]{1,0:T(8,128)}, f32[2048,512]{1,0:T(8,128)}), (f32[512,2048]{1,0:T(8,128)}, f32[2048,512]{1,0:T(8,128)})) %all-reduce.7.cloned.1.call-update) | async-done | bytes 8388624 | tf_op jit(solution)/shard_map/psum | solution.py:130
  198.8 0.0 all-reduce.9.cloned.1.call-update
  198.9 1.3 copy.21
  200.1 3.0 fusion.24
  203.2 0.3 fusion.23
  203.5 3.2 fusion.10
  206.7 8.4 %all-to-all-start.2 = ((f32[128,32,128]{2,1,0:T(8,128)}), f32[128,32,128]{2,1,0:T(8,128)}, u32[]{:S(2)}, u32[]{:S(2)}) async-start(f32[128,32,128]{2,1,0:T(8,128)} %bitcast.42), calls=%async_computation.2 | async-start | bytes 4194304 | tf_op jit(solution)/shard_map/all_to_all | solution.py:116
  215.1 0.5 broadcast.230
  215.7 0.8 reduce.3
  216.5 0.1 reshape.193
  216.6 138.0 %all-reduce = (f32[2048]{0:T(1024)S(1)}, f32[512]{0:T(512)S(1)}) all-reduce(f32[2048]{0:T(1024)S(1)} %get-tuple-element.56, f32[512]{0:T(512)S(1)} %get-tuple-element.29), channel_id=1, replica_groups=mesh['rows'=32,'cols'=4] {'rows'}, use_global_device_ids=true, to_apply=%region_8.9 | all-reduce | flops 2560 | bytes 20480 | tf_op jit(solution)/shard_map/psum | solution.py:130
  354.6 13.9 %all-reduce.2 = (f32[2048]{0:T(1024)S(1)}, f32[512]{0:T(512)S(1)}) all-reduce(f32[2048]{0:T(1024)S(1)} %get-tuple-element.31, f32[512]{0:T(512)S(1)} %get-tuple-element.32), channel_id=1, replica_groups=mesh['rows'=32,'cols'=4] {'cols'}, use_global_device_ids=true, to_apply=%region_9.10 | all-reduce | flops 2560 | bytes 20480 | tf_op jit(solution)/shard_map/psum | solution.py:130
  368.5 0.6 broadcast_multiply_fusion.3
  369.0 0.6 broadcast_multiply_fusion.2
  369.6 0.0 all-to-all-done.2
  369.6 25.4 %scatter_custom_fusion = f32[8192,128]{1,0:T(8,128)} fusion(s32[4096]{0:T(1024)S(1)} %bitcast.53, f32[4096,128]{1,0:T(8,128)} %bitcast.15, f32[]{:T(128)} %constant.40.clone.1), kind=kCustom, calls=%fused_computation.16 | custom fusion | flops 524288 | bytes 4194816 | tf_op jit(solution)/shard_map/scatter-add | solution.py:128
  395.0 4.9 %broadcast_multiply_fusion = f32[2048,512]{1,0:T(8,128)} fusion(f32[2048,512]{1,0:T(8,128)} %get-tuple-element.50), kind=kLoop, calls=%fused_computation.11 | loop fusion | flops 1048576 | bytes 8388608 | tf_op jit(solution)/shard_map/mul | solution.py:132
  399.9 2.3 broadcast_multiply_fusion.1
  (13 shorter events, 0.1 us)
Async XLA Ops:
  7.2 61.6 %copy-start = (bf16[512,2048]{1,0:T(8,128)(2,1)S(1)}, bf16[512,2048]{1,0:T(8,128)(2,1)}, u32[]{:S(2)}) copy-start(bf16[512,2048]{1,0:T(8,128)(2,1)} %param.11) | copy-start | bytes 6291460
  7.2 191.7 %all-reduce.7.cloned.1.call-start = ((), (), s32[]{:S(2)}) async-start(), calls=%async_computation.3 | async-start | bytes 16777216 | tf_op jit(solution)/shard_map/psum | solution.py:130
  43.8 25.0 %copy-start.4 = (f32[512]{0:T(512)S(1)}, f32[512]{0:T(512)}, u32[]{:S(2)}) copy-start(f32[512]{0:T(512)} %param.10) | copy-start | bytes 6148
  68.8 1.4 copy-start.3
  68.8 1.4 copy-start.6
  70.2 4.2 %copy-start.5 = (bf16[2048,512]{1,0:T(8,128)(2,1)S(1)}, bf16[2048,512]{1,0:T(8,128)(2,1)}, u32[]{:S(2)}) copy-start(bf16[2048,512]{1,0:T(8,128)(2,1)} %param.13) | copy-start | bytes 6291460
  78.0 1.3 copy-start.2
  82.7 312.4 %all-reduce.9.cloned.1.call-start = ((), (), s32[]{:S(2)}) async-start(), calls=%async_computation.4 | async-start | bytes 16777216 | tf_op jit(solution)/shard_map/psum | solution.py:130
  206.7 162.9 %all-to-all-start.2 = ((f32[128,32,128]{2,1,0:T(8,128)}), f32[128,32,128]{2,1,0:T(8,128)}, u32[]{:S(2)}, u32[]{:S(2)}) async-start(f32[128,32,128]{2,1,0:T(8,128)} %bitcast.42), calls=%async_computation.2 | async-start | bytes 4194304 | tf_op jit(solution)/shard_map/all_to_all | solution.py:116
  395.0 4.9 %copy-start.1 = (f32[512,2048]{1,0:T(8,128)S(1)}, f32[512,2048]{1,0:T(8,128)}, u32[]{:S(2)}) copy-start(f32[512,2048]{1,0:T(8,128)} %get-tuple-element.49) | copy-start | bytes 12582916
Sparse Core Ops, SparseCore 0:
  82.8 116.0 all-reduce.6
  201.6 183.0 all-reduce.8
